TPU v7x, 256 devices: a whole 4x4x8 slice. The times are simulated.
256 devices in a mesh: tm: 8 (over z), row: 8 (over x, core), obs: 4 (over y).
Axes of the slice: x: 4, y: 4, z: 8, core: 2. Of those that a mesh axis runs over, the one named last changes fastest.
Arguments:
- dyn_pattern: int32 [16, 8, 3], P('tm'), may hold values from 0 to 7
- dyn_values: float32 [16, 1024, 384], P('tm', ('row', 'obs')), may hold values from -0.3125 to 0.3125
- offsets: float32 [16, 1024], P('tm', ('row', 'obs')), may hold values from -6 to 6
- covariance: float32 [16, 1024, 1024], P('tm', ('row', 'obs')), may hold values from -1 to 14, as said below
- obs_block: int32 [16, 128], P('tm'), may hold values from 0 to 7
- obs_matrix: float32 [16, 128, 256], P('tm', 'obs'), may hold values from -0.375 to 0.375
- obs_data: float32 [16, 128], P('tm', 'obs'), may hold values from -6 to 6
Outputs:
- scan_dynamics: float32 [8, 1024, 1024], P('tm', ('row', 'obs'))
- scan_offset: float32 [8, 1024], P('tm', ('row', 'obs'))
- scan_covariance: float32 [8, 1024, 1024], P('tm', ('row', 'obs'))
- scan_factor: float32 [8, 1024, 512], P('tm', ('row', 'obs'))
- scan_information: float32 [8, 1024], P('tm', ('row', 'obs'))
Inputs may be any that keep to these rules, and one draw needn't show every extreme that they name: `dyn_pattern`: each entry names a block column. `obs_block`: each entry names a state block. Each covariance is symmetric and positive definite.
All inputs are finite; a program needn't handle non-finite values.
Results may differ from a plain program's by a relative error of at most 0.00019.
Values sent between devices are 32-bit elements; how exact they have to be, the bound alone decides.
A program may use at most 128 MiB of HBM per device.

v0:
```python
import jax
import jax.numpy as jnp
from jax import lax
from jax.sharding import PartitionSpec as P

largest_value = lax.Precision.HIGHEST


def shifted(block, axis, distance):
    devices = range(lax.axis_size(axis))
    route = [(i - distance, i) for i in devices if i - distance in devices]
    return lax.ppermute(block, axis, route)


def product(left, right):
    return jnp.dot(left, right, precision=largest_value, preferred_element_type=jnp.float32)


def lower_solve(lower, rhs):
    return lax.linalg.triangular_solve(lower, rhs, left_side=True, lower=True)


def assemble_dynamics(pattern, values):
    number_of_blocks = pattern.shape[0]
    per_row = pattern.shape[1]
    states = values.shape[0]
    block_extent = states // number_of_blocks
    indicator_matrix = (
        pattern[:, :, None] == jnp.arange(number_of_blocks, dtype=jnp.int32)[None, None, :]
    ).astype(jnp.float32)
    blocks = values.reshape(number_of_blocks, block_extent, per_row, block_extent)
    return jnp.einsum("ckd,cikj->cidj", indicator_matrix, blocks, precision=largest_value).reshape(
        states, states
    )


def assemble_factor(indices, matrix, number_of_blocks):
    item_count = matrix.shape[0]
    block_extent = matrix.shape[1] // 2
    reach = (indices[:, None] + jnp.arange(2, dtype=jnp.int32)[None, :]) % number_of_blocks
    indicator_matrix = (
        reach[:, :, None] == jnp.arange(number_of_blocks, dtype=jnp.int32)[None, None, :]
    ).astype(jnp.float32)
    piece_list = matrix.reshape(item_count, 2, block_extent)
    return jnp.einsum(
        "onr,onz->rzo", indicator_matrix, piece_list, precision=largest_value
    ).reshape(number_of_blocks * block_extent, item_count)


def combine(
    prior_dyn,
    prior_offsets,
    prior_cov,
    prior_factor,
    prior_zeta,
    own_dyn,
    own_offsets,
    own_cov,
    own_factor,
    own_zeta,
    row_start,
):
    panel_rows = prior_cov.shape[0]
    rank_width = own_factor.shape[1]
    own_pan = lax.dynamic_slice_in_dim(own_dyn, row_start, panel_rows, 0)
    gain_pan = product(prior_cov, own_factor)
    gain_rows = lax.all_gather(gain_pan, ("row", "obs"), axis=0, tiled=True)
    identity = jnp.eye(rank_width, dtype=jnp.float32)
    factor_pan = lax.dynamic_slice_in_dim(own_factor, row_start, panel_rows, 0)
    system = identity + lax.psum(product(factor_pan.T, gain_pan), ("row", "obs"))
    lower = jnp.linalg.cholesky(system)
    carried = product(own_dyn, gain_rows)
    observed = product(prior_dyn.T, own_factor)
    upper_part = lower_solve(lower, observed.T)
    weights = lower_solve(lower, carried.T).T
    weight_pan = lax.dynamic_slice_in_dim(weights, row_start, panel_rows, 0)
    spread_pan = product(prior_cov, own_dyn.T)
    moved = product(own_pan, lax.all_gather(spread_pan, ("row", "obs"), axis=0, tiled=True))
    new_dyn = product(own_pan, prior_dyn) - product(weight_pan, upper_part)
    new_cov = moved - product(weight_pan, weights.T) + own_cov
    residual = own_zeta - product(own_factor.T, prior_offsets)
    solved = lower_solve(lower, residual[:, None])[:, 0]
    new_offsets = product(own_pan, prior_offsets) + product(weight_pan, solved) + own_offsets
    upper_pan = lax.dynamic_slice_in_dim(upper_part, row_start, panel_rows, 1).T
    new_factor = jnp.concatenate([upper_pan, prior_factor], axis=1)
    new_zeta = jnp.concatenate([solved, prior_zeta])
    return (new_dyn, new_offsets, new_cov, new_factor, new_zeta)


def per_device(dyn_pattern, dyn_values, offsets, covariance, obs_block, obs_matrix, obs_data):
    panel_rows = covariance.shape[1]
    row_start = lax.axis_index(("row", "obs")) * panel_rows
    number_of_blocks = dyn_pattern.shape[1]
    obs_rows, obs_values = (
        lax.all_gather(obs_matrix, "obs", axis=1, tiled=True),
        lax.all_gather(obs_data, "obs", axis=1, tiled=True),
    )
    row_values, row_offsets = (
        lax.all_gather(dyn_values, ("row", "obs"), axis=1, tiled=True),
        lax.all_gather(offsets, ("row", "obs"), axis=1, tiled=True),
    )
    first_dyn = assemble_dynamics(dyn_pattern[0], row_values[0])
    second_dyn = assemble_dynamics(dyn_pattern[1], row_values[1])
    first_factor = assemble_factor(obs_block[0], obs_rows[0], number_of_blocks)
    second_factor = assemble_factor(obs_block[1], obs_rows[1], number_of_blocks)
    first_pan = lax.dynamic_slice_in_dim(first_factor, row_start, panel_rows, 0)
    dyn_pan, off_pan, cov_pan, fac_pan, zeta_full = combine(
        first_dyn,
        row_offsets[0],
        covariance[0],
        first_pan,
        obs_values[0],
        second_dyn,
        offsets[1],
        covariance[1],
        second_factor,
        obs_values[1],
        row_start,
    )
    later_pan, later_cov, later_off, later_fac, later_zeta = shifted(
        (dyn_pan, cov_pan, off_pan, fac_pan, zeta_full), "tm", -1
    )
    prior_full, later_full, later_factor, prior_offsets = (
        lax.all_gather(dyn_pan, ("row", "obs"), axis=0, tiled=True),
        lax.all_gather(later_pan, ("row", "obs"), axis=0, tiled=True),
        lax.all_gather(later_fac, ("row", "obs"), axis=0, tiled=True),
        lax.all_gather(off_pan, ("row", "obs"), axis=0, tiled=True),
    )
    top_dyn, top_off, top_cov, top_fac, top_zeta = combine(
        prior_full,
        prior_offsets,
        cov_pan,
        fac_pan,
        zeta_full,
        later_full,
        later_off,
        later_cov,
        later_factor,
        later_zeta,
        row_start,
    )
    even_turn = lax.axis_index("tm") % 2 == 0
    padded_fac = jnp.concatenate([fac_pan, jnp.zeros_like(fac_pan)], axis=1)
    padded_zeta = jnp.concatenate([zeta_full, jnp.zeros_like(zeta_full)])
    out_dyn = jnp.where(even_turn, top_dyn, dyn_pan)
    out_off = jnp.where(even_turn, top_off, off_pan)
    out_cov = jnp.where(even_turn, top_cov, cov_pan)
    out_fac = jnp.where(even_turn, top_fac, padded_fac)
    out_zeta = jnp.where(even_turn, top_zeta, padded_zeta)
    output_information = product(out_fac, out_zeta)
    return (out_dyn[None], out_off[None], out_cov[None], out_fac[None], output_information[None])


def solution(mesh):
    placed = (
        P("tm", None, None),
        P("tm", ("row", "obs"), None),
        P("tm", ("row", "obs")),
        P("tm", ("row", "obs"), None),
        P("tm", None),
        P("tm", "obs", None),
        P("tm", "obs"),
    )
    return jax.shard_map(
        per_device,
        mesh=mesh,
        in_specs=placed,
        out_specs=(
            P("tm", ("row", "obs"), None),
            P("tm", ("row", "obs")),
            P("tm", ("row", "obs"), None),
            P("tm", ("row", "obs"), None),
            P("tm", ("row", "obs")),
        ),
        check_vma=False,
    )
```

profile of v0, /device:TPU:1, one launch (start us, length us, event | category | flops | bytes accessed | tf_op | source)
XLA Modules:
  0.0 616.6 jit_solution(8064863237237655006)
XLA Ops:
  8.0 11.5 %all_gather.37 = f32[2,128,256]{2,1,0:T(8,128)S(1)} all-gather(f32[2,32,256]{2,1,0:T(8,128)} %param.16), channel_id=1, replica_groups=mesh['tm'=8,'row'=8,'obs'=4] {'obs'}, dimensions={1}, use_global_device_ids=true | all-gather | bytes 327680 | tf_op jit(solution)/shard_map/all_gather | solution.py:95
  24.0 40.9 %all-gather.10.cloned.1.call-done = f32[2,1024,384]{2,1,0:T(8,128)} async-done(((f32[2,32,384]{2,1,0:T(8,128)}), f32[2,1024,384]{2,1,0:T(8,128)}) %all-gather.10.cloned.1.call-update) | async-done | bytes 3145744 | tf_op jit(solution)/shard_map/all_gather | solution.py:99
  64.9 3.2 fusion.135
  68.2 3.6 reshape.312
  71.8 4.3 fusion.104
  78.1 4.9 convolution_bitcast_fusion.1
  84.7 89.2 %all-reduce.5.cloned.1.call-done = f32[128,128]{1,0:T(8,128)} async-done(((f32[128,128]{1,0:T(8,128)}), f32[128,128]{1,0:T(8,128)}) %all-reduce.5.cloned.1.call-update) | async-done | bytes 65552 | tf_op jit(solution)/shard_map/psum | solution.py:70
  175.6 11.7 %cholesky.60 = f32[128,128]{1,0:T(8,128)S(1)} custom-call(f32[128,128]{1,0:T(8,128)S(1)} %fusion.77), custom_call_target="Cholesky" | custom-call | tf_op jit(solution)/shard_map/jit(cholesky)/cholesky | solution.py:71
  188.7 9.8 %custom-call.31 = f32[1,128,128]{1,2,0:T(8,128)S(1)} custom-call(f32[1,128,128]{2,1,0:T(8,128)S(1)} %fusion.55), custom_call_target="InvertDiagBlocksLowerTriangular" | custom-call | tf_op jit(solution)/shard_map/triangular_solve/custom-call.4 | solution.py:20
  200.7 4.3 fusion.107
  207.1 3.0 fusion
  212.1 3.8 collective-permute-done.1
  216.6 42.6 %all_gather.38 = f32[1024,128]{1,0:T(8,128)S(1)} all-gather(f32[32,128]{1,0:T(8,128)S(1)} %bitcast.273), channel_id=1, replica_groups=mesh['tm'=8,'row'=8,'obs'=4] {'row','obs'}, dimensions={0}, use_global_device_ids=true | all-gather | bytes 540672 | tf_op jit(solution)/shard_map/all_gather | solution.py:67
  259.2 3.4 copy.79
  262.6 4.8 fusion.133
  273.0 4.4 collective-permute-done
  278.9 4.8 fusion.52
  288.9 40.2 %all-gather = f32[32,32,2]{1,2,0:T(2,128)S(1)} all-gather(f32[1,32,2]{1,2,0:T(2,128)S(1)} %bitcast.282), channel_id=1, replica_groups=mesh['tm'=8,'row'=8,'obs'=4] {'row','obs'}, dimensions={0}, use_global_device_ids=true | all-gather | bytes 8448 | tf_op jit(solution)/shard_map/all_gather | solution.py:100
  329.1 5.2 all-gather.1
  335.7 6.7 %fusion.141 = f32[32,1024]{1,0:T(8,128)} fusion(f32[32,1024]{1,0:T(8,128)S(1)} %fusion.12, f32[1024,1024]{1,0:T(8,128)} %all-gather.12.cloned.1.call-done), kind=kOutput, calls=%fused_computation.205 | convolution fusion | flops 402653184 | bytes 4456448 | tf_op jit(solution)/shard_map/dot_general | solution.py:16
  348.2 63.2 %all-reduce.1 = f32[1024]{0:T(1024)S(1)} all-reduce(f32[1024]{0:T(1024)S(1)} %dynamic-update-slice.17), channel_id=1, replica_groups=mesh['tm'=8,'row'=8,'obs'=4] {'row','obs'}, use_global_device_ids=true, to_apply=%add.1 | all-reduce | flops 1024 | bytes 8192
  413.4 6.0 fusion.140
  419.4 80.5 %all-reduce.7.cloned.1.call-done = f32[256,256]{0,1:T(8,128)} async-done(((f32[256,256]{0,1:T(8,128)}), f32[256,256]{0,1:T(8,128)}) %all-reduce.7.cloned.1.call-update) | async-done | bytes 262160 | tf_op jit(solution)/shard_map/psum | solution.py:70
  502.0 11.7 %cholesky.115 = f32[128,128]{1,0:T(8,128)S(1)} custom-call(f32[128,128]{1,0:T(8,128)S(1)} %cholesky.141), custom_call_target="Cholesky" | custom-call | tf_op jit(solution)/shard_map/jit(cholesky)/cholesky | solution.py:71
  513.8 9.8 %custom-call.26 = f32[1,128,128]{1,2,0:T(8,128)S(1)} custom-call(f32[1,128,128]{2,1,0:T(8,128)S(1)} %get-tuple-element.62), custom_call_target="InvertDiagBlocksLowerTriangular" | custom-call | tf_op jit(solution)/shard_map/jit(cholesky)/cholesky | solution.py:71
  524.1 11.7 %cholesky.128 = f32[128,128]{1,0:T(8,128)S(1)} custom-call(f32[128,128]{1,0:T(8,128)S(1)} %convolution_subtract_fusion.3), custom_call_target="Cholesky" | custom-call | tf_op jit(solution)/shard_map/jit(cholesky)/cholesky | solution.py:71
  538.5 4.0 while.5
  542.5 19.8 %custom-call.33 = f32[2,128,128]{1,2,0:T(8,128)S(1)} custom-call(f32[2,128,128]{2,1,0:T(8,128)S(1)} %get-tuple-element.29), custom_call_target="InvertDiagBlocksLowerTriangular" | custom-call | tf_op jit(solution)/shard_map/triangular_solve/custom-call.5 | solution.py:20
  566.5 9.2 %fusion.139 = f32[256,1024]{1,0:T(8,128)S(1)} fusion(f32[1024,256]{1,0:T(8,128)} %all-gather.20.cloned.1.call-done, f32[1024,1024]{1,0:T(8,128)} %all-gather.12.cloned.1.call-done), kind=kOutput, calls=%fused_computation.203 | convolution fusion | flops 3221225472 | bytes 6291456 | tf_op jit(solution)/shard_map/dot_general | solution.py:16
  579.2 4.1 fusion.14
  585.1 19.4 %all-gather.22.cloned.1.call-done = f32[1024,1024]{1,0:T(8,128)} async-done(((f32[32,1024]{1,0:T(8,128)}), f32[1024,1024]{1,0:T(8,128)}) %all-gather.22.cloned.1.call-update) | async-done | bytes 4194320 | tf_op jit(solution)/shard_map/all_gather | solution.py:78
  604.5 5.4 fusion.11
  (159 shorter events, 56.9 us)
Async XLA Ops:
  7.2 16.8 %copy-start.15 = (s32[2,8,3]{1,0,2:T(2,128)S(1)}, s32[2,8,3]{1,0,2:T(2,128)}, u32[]{:S(2)}) copy-start(s32[2,8,3]{1,0,2:T(2,128)} %param.11) | copy-start | bytes 580
  7.2 57.8 %all-gather.10.cloned.1.call-start = ((), (), s32[]{:S(2)}) async-start(), calls=%async_computation | async-start | bytes 3244032 | tf_op jit(solution)/shard_map/all_gather | solution.py:99
  7.9 165.9 %all-reduce.5.cloned.1.call-start = ((), (), s32[]{:S(2)}) async-start(), calls=%async_computation.1 | async-start | bytes 131072 | tf_op jit(solution)/shard_map/psum | solution.py:70
  23.9 255.0 %all-gather.18.cloned.1.call-start = ((), (), s32[]{:S(2)}) async-start(), calls=%async_computation.5 | async-start | bytes 4325376 | tf_op jit(solution)/shard_map/all_gather | solution.py:78
  68.2 9.9 %copy-start.10 = (f32[2,32,1024]{2,1,0:T(8,128)S(1)}, f32[2,32,1024]{2,1,0:T(8,128)}, u32[]{:S(2)}) copy-start(f32[2,32,1024]{2,1,0:T(8,128)} %param.14) | copy-start | bytes 786436
  76.1 2.0 copy-start
  83.0 201.2 %all-gather.16.cloned.1.call-start = ((), (), s32[]{:S(2)}) async-start(), calls=%async_computation.4 | async-start | bytes 1081344 | tf_op jit(solution)/shard_map/all_gather | solution.py:126
  84.6 120.4 %copy-start.9 = (f32[8,128,128]{2,1,0:T(8,128)}, f32[8,128,128]{2,1,0:T(8,128)S(1)}, u32[]{:S(2)}) copy-start(f32[8,128,128]{2,1,0:T(8,128)S(1)} %copy.56) | copy-start | bytes 1572868
  205.0 2.0 copy-start.2
  210.9 5.0 collective-permute-start.1
  215.9 0.6 copy-start.13
  216.5 119.2 %all-gather.12.cloned.1.call-start = ((), (), s32[]{:S(2)}) async-start(), calls=%async_computation.2 | async-start | bytes 4325376 | tf_op jit(solution)/shard_map/all_gather | solution.py:125
  259.2 3.5 copy-start.1
  262.6 5.9 copy-start.6
  262.6 5.9 copy-start.3
  271.5 6.6 %copy-start.7 = (f32[32,1024]{1,0:T(8,128)}, f32[32,1024]{1,0:T(8,128)S(1)}, u32[]{:S(2)}) copy-start(f32[32,1024]{1,0:T(8,128)S(1)} %fusion.6) | copy-start | bytes 393220
  271.5 17.3 %copy-start.14 = (f32[2,32]{1,0:T(2,128)S(1)}, f32[2,32]{1,0:T(2,128)}, u32[]{:S(2)}) copy-start(f32[2,32]{1,0:T(2,128)} %param.13) | copy-start | bytes 772
  271.5 57.6 %copy-start.16 = (f32[2,32]{1,0:T(2,128)S(1)}, f32[2,32]{1,0:T(2,128)}, u32[]{:S(2)}) copy-start(f32[2,32]{1,0:T(2,128)} %param.17) | copy-start | bytes 772
  271.5 5.8 collective-permute-start
  277.4 0.7 copy-start.12
  278.1 135.3 %all-gather.14.cloned.1.call-start = ((), (), s32[]{:S(2)}) async-start(), calls=%async_computation.3 | async-start | bytes 4325376 | tf_op jit(solution)/shard_map/all_gather | solution.py:124
  278.6 221.2 %all-reduce.7.cloned.1.call-start = ((), (), s32[]{:S(2)}) async-start(), calls=%async_computation.6 | async-start | bytes 524288 | tf_op jit(solution)/shard_map/psum | solution.py:70
  283.7 58.8 %copy-start.17 = (u32[256]{0:T(256)S(1)}, u32[256]{0:T(256)}, u32[]{:S(2)}) copy-start(u32[256]{0:T(256)} %constant.217) | copy-start | bytes 3076
  284.2 127.2 %copy-start.5 = (f32[1024,256]{1,0:T(8,128)S(1)}, f32[1024,256]{1,0:T(8,128)}, u32[]{:S(2)}) copy-start(f32[1024,256]{1,0:T(8,128)} %all-gather.16.cloned.1.call-done) | copy-start | bytes 3145732
  286.1 2.0 copy-start.11
  288.1 278.4 %all-gather.20.cloned.1.call-start = ((), (), s32[]{:S(2)}) async-start(), calls=%async_computation.7 | async-start | bytes 1081344 | tf_op jit(solution)/shard_map/all_gather | solution.py:67
  288.8 315.7 %all-gather.22.cloned.1.call-start = ((), (), s32[]{:S(2)}) async-start(), calls=%async_computation.8 | async-start | bytes 4325376 | tf_op jit(solution)/shard_map/all_gather | solution.py:78
  343.9 68.2 %collective-permute-start.2 = (f32[256]{0:T(256)S(1)}, f32[256]{0:T(256)S(1)}, u32[]{:S(2)}, u32[]{:S(2)}) collective-permute-start(f32[256]{0:T(256)S(1)} %pad_maximum_fusion.5), channel_id=1, source_target_pairs={{32,0},{64,32},{96,64},{128,96},{160,128},{192,160},{224,192},{33,... | collective-permute-start | bytes 3080 | tf_op jit(solution)/shard_map/ppermute | solution.py:12
  346.6 236.8 %collective-permute-start.3 = (f32[32]{0:T(128)S(1)}, f32[32]{0:T(128)S(1)}, u32[]{:S(2)}, u32[]{:S(2)}) collective-permute-start(f32[32]{0:T(128)S(1)} %fusion.16), channel_id=1, source_target_pairs={{32,0},{64,32},{96,64},{128,96},{160,128},{192,160},{224,192},{33,... | collective-permute-start | bytes 392 | tf_op jit(solution)/shard_map/ppermute | solution.py:12
  412.1 173.0 %collective-permute-start.4 = (f32[32,1024]{1,0:T(8,128)S(1)}, f32[32,1024]{1,0:T(8,128)S(1)}, u32[]{:S(2)}, u32[]{:S(2)}) collective-permute-start(f32[32,1024]{1,0:T(8,128)S(1)} %fusion.12), channel_id=1, source_target_pairs={{32,0},{64,32},{96,64},{128,96},{160,128},{192,160},{224,192},{33,... | collective-permute-start | bytes 393224 | tf_op jit(solution)/shard_map/ppermute | solution.py:12
  575.7 3.5 copy-start.4
  575.7 3.5 copy-start.8
Sparse Core Ops, SparseCore 0:
  10.6 54.3 all-gather.9
  68.8 104.9 all-reduce.4
  177.3 50.7 all-gather.17
  231.4 47.2 all-gather.15
  281.4 50.4 all-gather.11
  335.2 50.5 all-gather.13
  389.4 110.4 all-reduce.6
  503.0 48.6 all-gather.19
  554.3 50.1 all-gather.21
where the time goes:
time: 624 us; the launch traced here: 617 us
  waiting for transfers between devices  240 us (38%)
  blocking collectives  163 us (26%)
  other arithmetic  82 us (13%)
  matrix products  81.8 us (13%)
  local copies, waits for them, and re-layouts  25.7 us (4%)
  between operations  16.7 us (3%)
  starting transfers between devices  7.45 us (1%)
    psum x2, waiting for transfers between devices, combine(): lax.psum(product(factor_pan.T, gain_pan), ('row', 'obs'))  170 us
    dot_general x25, matrix products, product(): jnp.dot(left, right, precision=largest_value, preferred_element_type=jnp....  65.3 us
    unnamed x1, blocking collectives  63.2 us
    another operation x10, other arithmetic, combine(): lower = jnp.linalg.cholesky(system)  47 us
    all_gather x1, blocking collectives, combine(): gain_rows = lax.all_gather(gain_pan, ('row', 'obs'), axis=0, tiled=True)  42.6 us
    all_gather x1, waiting for transfers between devices, per_device(): lax.all_gather(dyn_values, ('row', 'obs'), axis=1, tiled=True)  40.9 us
    all_gather x1, blocking collectives, per_device(): lax.all_gather(offsets, ('row', 'obs'), axis=1, tiled=True)  40.2 us
    another operation x8, other arithmetic, lower_solve(): return lax.linalg.triangular_solve(lower, rhs, left_side=True, lower=True)  30.5 us
  transfers between devices with their start and end apart: 14, of which 6 were waited for; matrix products, arithmetic and copies ran while one was open for 29% of the time, Pallas kernels for 0%

commit v1 on v0

--- a/solution.py
+++ b/solution.py
@@ -67,7 +67,7 @@
     gain_rows = lax.all_gather(gain_pan, ("row", "obs"), axis=0, tiled=True)
     identity = jnp.eye(rank_width, dtype=jnp.float32)
     factor_pan = lax.dynamic_slice_in_dim(own_factor, row_start, panel_rows, 0)
-    system = identity + lax.psum(product(factor_pan.T, gain_pan), ("row", "obs"))
+    system = identity + lax.psum(lax.psum(product(factor_pan.T, gain_pan), "row"), "obs")
     lower = jnp.linalg.cholesky(system)
     carried = product(own_dyn, gain_rows)
     observed = product(prior_dyn.T, own_factor)

time: 624 us -> 560 us (0.90)
  the two profiles are of different devices: /device:TPU:1 before, /device:TPU:232 now
where the time goes in v1:
time: 560 us; the launch traced here: 553 us
  blocking collectives  168 us (30%)
  waiting for transfers between devices  158 us (28%)
  other arithmetic  82.1 us (15%)
  matrix products  81.8 us (15%)
  local copies, waits for them, and re-layouts  25.8 us (5%)
  starting transfers between devices  18.3 us (3%)
  between operations  18.2 us (3%)
    psum x2, waiting for transfers between devices, combine(): lax.psum(product(factor_pan.T, gain_pan), 'row')  129 us
    dot_general x25, matrix products, product(): jnp.dot(left, right, precision=largest_value, preferred_element_type=jnp....  65.3 us
    unnamed x1, blocking collectives  64.7 us
    another operation x10, other arithmetic, combine(): lower = jnp.linalg.cholesky(system)  47 us
    all_gather x1, blocking collectives, combine(): gain_rows = lax.all_gather(gain_pan, ('row', 'obs'), axis=0, tiled=True)  43.2 us
    all_gather x1, blocking collectives, per_device(): lax.all_gather(offsets, ('row', 'obs'), axis=1, tiled=True)  39 us
    another operation x8, other arithmetic, lower_solve(): return lax.linalg.triangular_solve(lower, rhs, left_side=True, lower=True)  30.5 us
    psum x2, waiting for transfers between devices, combine(): lax.psum(lax.psum(product(factor_pan.T, gain_pan), 'row'), 'obs')  25.9 us
  transfers between devices with their start and end apart: 16, of which 4 were waited for; matrix products, arithmetic and copies ran while one was open for 32% of the time, Pallas kernels for 0%

profile of v1, /device:TPU:232, one launch (start us, length us, event | category | flops | bytes accessed | tf_op | source)
XLA Modules:
  0.0 552.6 jit_solution(4020470200545868204)
XLA Ops:
  8.8 12.7 %all_gather.37 = f32[2,128,256]{2,1,0:T(8,128)S(1)} all-gather(f32[2,32,256]{2,1,0:T(8,128)} %param.16), channel_id=1, replica_groups=mesh['tm'=8,'row'=8,'obs'=4] {'obs'}, dimensions={1}, use_global_device_ids=true | all-gather | bytes 327680 | tf_op jit(solution)/shard_map/all_gather | solution.py:95
  26.0 64.2 %all-reduce.7.cloned.1.call-done = f32[128,128]{1,0:T(8,128)} async-done(((f32[128,128]{1,0:T(8,128)}), f32[128,128]{1,0:T(8,128)}) %all-reduce.7.cloned.1.call-update) | async-done | bytes 65552 | tf_op jit(solution)/shard_map/psum | solution.py:70
  93.5 3.6 reshape.312
  97.2 4.3 fusion.104
  103.5 4.9 convolution_bitcast_fusion.1
  110.1 25.9 %all-reduce.9.cloned.1.call-done = f32[128,128]{1,0:T(8,128)} async-done(((f32[128,128]{1,0:T(8,128)}), f32[128,128]{1,0:T(8,128)}) %all-reduce.9.cloned.1.call-update) | async-done | bytes 65552 | tf_op jit(solution)/shard_map/psum | solution.py:70
  137.8 11.7 %cholesky.60 = f32[128,128]{1,0:T(8,128)S(1)} custom-call(f32[128,128]{1,0:T(8,128)S(1)} %fusion.77), custom_call_target="Cholesky" | custom-call | tf_op jit(solution)/shard_map/jit(cholesky)/cholesky | solution.py:71
  150.9 9.8 %custom-call.31 = f32[1,128,128]{1,2,0:T(8,128)S(1)} custom-call(f32[1,128,128]{2,1,0:T(8,128)S(1)} %fusion.55), custom_call_target="InvertDiagBlocksLowerTriangular" | custom-call | tf_op jit(solution)/shard_map/triangular_solve/custom-call.4 | solution.py:20
  162.9 4.3 fusion.107
  173.0 3.3 collective-permute-start.1
  178.5 43.2 %all_gather.38 = f32[1024,128]{1,0:T(8,128)S(1)} all-gather(f32[32,128]{1,0:T(8,128)S(1)} %bitcast.273), channel_id=1, replica_groups=mesh['tm'=8,'row'=8,'obs'=4] {'row','obs'}, dimensions={0}, use_global_device_ids=true | all-gather | bytes 540672 | tf_op jit(solution)/shard_map/all_gather | solution.py:67
  221.8 3.4 copy.79
  225.3 4.8 fusion.133
  234.2 4.3 collective-permute-start
  238.5 4.8 fusion.52
  249.2 64.4 %all-reduce.11.cloned.1.call-done = f32[256,256]{0,1:T(8,128)} async-done(((f32[256,256]{0,1:T(8,128)}), f32[256,256]{0,1:T(8,128)}) %all-reduce.11.cloned.1.call-update) | async-done | bytes 262160 | tf_op jit(solution)/shard_map/psum | solution.py:70
  314.4 39.0 %all-gather = f32[32,32,2]{1,2,0:T(2,128)S(1)} all-gather(f32[1,32,2]{1,2,0:T(2,128)S(1)} %bitcast.282), channel_id=1, replica_groups=mesh['tm'=8,'row'=8,'obs'=4] {'row','obs'}, dimensions={0}, use_global_device_ids=true | all-gather | bytes 8448 | tf_op jit(solution)/shard_map/all_gather | solution.py:100
  353.5 8.5 %all-gather.1 = f32[4,32,2]{1,2,0:T(2,128)S(1)} all-gather(f32[1,32,2]{1,2,0:T(2,128)S(1)} %bitcast.288), channel_id=1, replica_groups=mesh['tm'=8,'row'=8,'obs'=4] {'obs'}, dimensions={0}, use_global_device_ids=true | all-gather | bytes 1280 | tf_op jit(solution)/shard_map/all_gather | solution.py:96
  363.3 6.7 %fusion.141 = f32[32,1024]{1,0:T(8,128)} fusion(f32[32,1024]{1,0:T(8,128)S(1)} %fusion.12, f32[1024,1024]{1,0:T(8,128)} %all-gather.12.cloned.1.call-done), kind=kOutput, calls=%fused_computation.205 | convolution fusion | flops 402653184 | bytes 4456448 | tf_op jit(solution)/shard_map/dot_general | solution.py:16
  371.5 3.3 collective-permute-start.2
  376.2 3.3 collective-permute-start.3
  379.8 64.7 %all-reduce.1 = f32[1024]{0:T(1024)S(1)} all-reduce(f32[1024]{0:T(1024)S(1)} %dynamic-update-slice.17), channel_id=1, replica_groups=mesh['tm'=8,'row'=8,'obs'=4] {'row','obs'}, use_global_device_ids=true, to_apply=%add.1 | all-reduce | flops 1024 | bytes 8192
  445.1 3.4 collective-permute-start.4
  448.6 6.0 %fusion.140 = f32[256,1024]{1,0:T(8,128)S(1)} fusion(f32[1024,256]{1,0:T(8,128)S(1)} %copy-done.5, f32[1024,1024]{1,0:T(8,128)} %all-gather.14.cloned.1.call-done), kind=kOutput, calls=%fused_computation.204 | convolution fusion | flops 3221225472 | bytes 6291456 | tf_op jit(solution)/shard_map/dot_general | solution.py:16
  456.7 11.7 %cholesky.115 = f32[128,128]{1,0:T(8,128)S(1)} custom-call(f32[128,128]{1,0:T(8,128)S(1)} %cholesky.141), custom_call_target="Cholesky" | custom-call | tf_op jit(solution)/shard_map/jit(cholesky)/cholesky | solution.py:71
  468.5 9.8 %custom-call.26 = f32[1,128,128]{1,2,0:T(8,128)S(1)} custom-call(f32[1,128,128]{2,1,0:T(8,128)S(1)} %get-tuple-element.62), custom_call_target="InvertDiagBlocksLowerTriangular" | custom-call | tf_op jit(solution)/shard_map/jit(cholesky)/cholesky | solution.py:71
  478.8 11.7 %cholesky.128 = f32[128,128]{1,0:T(8,128)S(1)} custom-call(f32[128,128]{1,0:T(8,128)S(1)} %convolution_subtract_fusion.3), custom_call_target="Cholesky" | custom-call | tf_op jit(solution)/shard_map/jit(cholesky)/cholesky | solution.py:71
  493.2 4.0 while.5
  497.2 19.8 %custom-call.33 = f32[2,128,128]{1,2,0:T(8,128)S(1)} custom-call(f32[2,128,128]{2,1,0:T(8,128)S(1)} %get-tuple-element.29), custom_call_target="InvertDiagBlocksLowerTriangular" | custom-call | tf_op jit(solution)/shard_map/triangular_solve/custom-call.5 | solution.py:20
  521.2 9.2 %fusion.139 = f32[256,1024]{1,0:T(8,128)S(1)} fusion(f32[1024,256]{1,0:T(8,128)} %all-gather.20.cloned.1.call-done, f32[1024,1024]{1,0:T(8,128)} %all-gather.12.cloned.1.call-done), kind=kOutput, calls=%fused_computation.203 | convolution fusion | flops 3221225472 | bytes 6291456 | tf_op jit(solution)/shard_map/dot_general | solution.py:16
  533.9 4.1 fusion.14
  539.8 5.4 fusion.11
  (165 shorter events, 58.2 us)
Async XLA Ops:
  8.0 17.9 %copy-start.15 = (s32[2,8,3]{1,0,2:T(2,128)S(1)}, s32[2,8,3]{1,0,2:T(2,128)}, u32[]{:S(2)}) copy-start(s32[2,8,3]{1,0,2:T(2,128)} %param.11) | copy-start | bytes 580
  8.0 82.2 %all-reduce.7.cloned.1.call-start = ((), (), s32[]{:S(2)}) async-start(), calls=%async_computation.1 | async-start | bytes 131072 | tf_op jit(solution)/shard_map/psum | solution.py:70
  25.2 65.0 %all-gather.10.cloned.1.call-start = ((), (), s32[]{:S(2)}) async-start(), calls=%async_computation | async-start | bytes 3244032 | tf_op jit(solution)/shard_map/all_gather | solution.py:99
  25.8 110.2 %all-reduce.9.cloned.1.call-start = ((), (), s32[]{:S(2)}) async-start(), calls=%async_computation.2 | async-start | bytes 131072 | tf_op jit(solution)/shard_map/psum | solution.py:70
  90.2 148.3 %all-gather.18.cloned.1.call-start = ((), (), s32[]{:S(2)}) async-start(), calls=%async_computation.6 | async-start | bytes 4325376 | tf_op jit(solution)/shard_map/all_gather | solution.py:78
  93.5 9.9 %copy-start.10 = (f32[2,32,1024]{2,1,0:T(8,128)S(1)}, f32[2,32,1024]{2,1,0:T(8,128)}, u32[]{:S(2)}) copy-start(f32[2,32,1024]{2,1,0:T(8,128)} %param.14) | copy-start | bytes 786436
  101.4 2.0 copy-start
  108.4 135.4 %all-gather.16.cloned.1.call-start = ((), (), s32[]{:S(2)}) async-start(), calls=%async_computation.5 | async-start | bytes 1081344 | tf_op jit(solution)/shard_map/all_gather | solution.py:126
  110.1 57.2 %copy-start.9 = (f32[8,128,128]{2,1,0:T(8,128)}, f32[8,128,128]{2,1,0:T(8,128)S(1)}, u32[]{:S(2)}) copy-start(f32[8,128,128]{2,1,0:T(8,128)S(1)} %copy.56) | copy-start | bytes 1572868
  167.2 2.0 copy-start.2
  173.0 4.9 collective-permute-start.1
  178.5 135.1 %all-reduce.11.cloned.1.call-start = ((), (), s32[]{:S(2)}) async-start(), calls=%async_computation.7 | async-start | bytes 524288 | tf_op jit(solution)/shard_map/psum | solution.py:70
  221.8 3.5 copy-start.1
  225.3 5.9 %copy-start.6 = (f32[128,8,8,128]{3,1,2,0:T(8,128)}, f32[128,8,8,128]{3,1,2,0:T(8,128)S(1)}, u32[]{:S(2)}) copy-start(f32[128,8,8,128]{3,1,2,0:T(8,128)S(1)} %copy.79) | copy-start | bytes 12582916
  225.3 5.9 %copy-start.3 = (f32[8,8,128,128]{3,1,2,0:T(8,128)S(1)}, f32[8,8,128,128]{3,1,2,0:T(8,128)}, u32[]{:S(2)}) copy-start(f32[8,8,128,128]{3,1,2,0:T(8,128)} %copy-done.2) | copy-start | bytes 12582916
  234.2 14.2 %copy-start.7 = (f32[32,1024]{1,0:T(8,128)}, f32[32,1024]{1,0:T(8,128)S(1)}, u32[]{:S(2)}) copy-start(f32[32,1024]{1,0:T(8,128)S(1)} %fusion.6) | copy-start | bytes 393220
  234.2 80.2 %copy-start.14 = (f32[2,32]{1,0:T(2,128)S(1)}, f32[2,32]{1,0:T(2,128)}, u32[]{:S(2)}) copy-start(f32[2,32]{1,0:T(2,128)} %param.13) | copy-start | bytes 772
  234.2 119.3 %copy-start.16 = (f32[2,32]{1,0:T(2,128)S(1)}, f32[2,32]{1,0:T(2,128)}, u32[]{:S(2)}) copy-start(f32[2,32]{1,0:T(2,128)} %param.17) | copy-start | bytes 772
  234.2 13.5 %collective-permute-start = (f32[32,1024]{1,0:T(8,128)S(1)}, f32[32,1024]{1,0:T(8,128)S(1)}, u32[]{:S(2)}, u32[]{:S(2)}) collective-permute-start(f32[32,1024]{1,0:T(8,128)S(1)} %fusion.6), channel_id=1, source_target_pairs={{32,0},{64,32},{96,64},{128,96},{160,128},{192,160},{224,192},{33,... | collective-permute-start | bytes 393224 | tf_op jit(solution)/shard_map/ppermute | solution.py:12
  243.3 126.8 %copy-start.17 = (u32[256]{0:T(256)S(1)}, u32[256]{0:T(256)}, u32[]{:S(2)}) copy-start(u32[256]{0:T(256)} %constant.217) | copy-start | bytes 3076
  243.8 200.7 %copy-start.5 = (f32[1024,256]{1,0:T(8,128)S(1)}, f32[1024,256]{1,0:T(8,128)}, u32[]{:S(2)}) copy-start(f32[1024,256]{1,0:T(8,128)} %all-gather.16.cloned.1.call-done) | copy-start | bytes 3145732
  245.7 68.0 %copy-start.11 = (f32[32,256]{1,0:T(8,128)}, f32[32,256]{1,0:T(8,128)S(1)}, u32[]{:S(2)}) copy-start(f32[32,256]{1,0:T(8,128)S(1)} %fusion.138) | copy-start | bytes 98308
  247.6 115.7 %all-gather.12.cloned.1.call-start = ((), (), s32[]{:S(2)}) async-start(), calls=%async_computation.3 | async-start | bytes 4325376 | tf_op jit(solution)/shard_map/all_gather | solution.py:125
  248.4 200.2 %all-gather.14.cloned.1.call-start = ((), (), s32[]{:S(2)}) async-start(), calls=%async_computation.4 | async-start | bytes 4325376 | tf_op jit(solution)/shard_map/all_gather | solution.py:124
  249.1 205.5 %all-reduce.13.cloned.1.call-start = ((), (), s32[]{:S(2)}) async-start(), calls=%async_computation.8 | async-start | bytes 524288 | tf_op jit(solution)/shard_map/psum | solution.py:70
  313.6 207.6 %all-gather.20.cloned.1.call-start = ((), (), s32[]{:S(2)}) async-start(), calls=%async_computation.9 | async-start | bytes 1081344 | tf_op jit(solution)/shard_map/all_gather | solution.py:67
  314.4 225.4 %all-gather.22.cloned.1.call-start = ((), (), s32[]{:S(2)}) async-start(), calls=%async_computation.10 | async-start | bytes 4325376 | tf_op jit(solution)/shard_map/all_gather | solution.py:78
  371.5 73.6 %collective-permute-start.2 = (f32[256]{0:T(256)S(1)}, f32[256]{0:T(256)S(1)}, u32[]{:S(2)}, u32[]{:S(2)}) collective-permute-start(f32[256]{0:T(256)S(1)} %pad_maximum_fusion.5), channel_id=1, source_target_pairs={{32,0},{64,32},{96,64},{128,96},{160,128},{192,160},{224,192},{33,... | collective-permute-start | bytes 3080 | tf_op jit(solution)/shard_map/ppermute | solution.py:12
  376.2 161.9 %collective-permute-start.3 = (f32[32]{0:T(128)S(1)}, f32[32]{0:T(128)S(1)}, u32[]{:S(2)}, u32[]{:S(2)}) collective-permute-start(f32[32]{0:T(128)S(1)} %fusion.16), channel_id=1, source_target_pairs={{32,0},{64,32},{96,64},{128,96},{160,128},{192,160},{224,192},{33,... | collective-permute-start | bytes 392 | tf_op jit(solution)/shard_map/ppermute | solution.py:12
  445.1 94.7 %collective-permute-start.4 = (f32[32,1024]{1,0:T(8,128)S(1)}, f32[32,1024]{1,0:T(8,128)S(1)}, u32[]{:S(2)}, u32[]{:S(2)}) collective-permute-start(f32[32,1024]{1,0:T(8,128)S(1)} %fusion.12), channel_id=1, source_target_pairs={{32,0},{64,32},{96,64},{128,96},{160,128},{192,160},{224,192},{33,... | collective-permute-start | bytes 393224 | tf_op jit(solution)/shard_map/ppermute | solution.py:12
  530.4 3.5 copy-start.4
  530.4 3.5 copy-start.8
  (2 other events, 1.3 us)
Sparse Core Ops, SparseCore 0:
  25.4 64.7 all-reduce.6
  92.6 43.3 all-reduce.8
  247.7 65.8 all-reduce.10
  315.9 46.1 all-reduce.12
Sparse Core Ops, SparseCore 1:
  28.3 49.8 all-gather.9
  108.5 49.8 all-gather.17
  178.6 50.1 all-gather.15
  251.5 51.5 all-gather.11
  306.3 51.2 all-gather.13
  360.1 47.6 all-gather.19
  410.1 50.9 all-gather.21
